TPU v7x, 32 devices: a whole 2x2x4 slice. The times are simulated.
32 devices in a mesh: dp: 4 (over z), tensor: 8 (over y, x, core).
Axes of the slice: x: 2, y: 2, z: 4, core: 2. Of those that a mesh axis runs over, the one named last changes fastest.
Arguments:
- hidden_in: bfloat16 [4, 1024, 2304], P('dp', 'tensor'), may hold values from -6 to 6
- prompt_len: int32 [4], P('dp'), may hold values from 1 to 1024, 2560 in all
- start_pos: int32 [4], P('dp'), may hold values from 0 to 511
- routes: int32 [4, 1024, 2], P('dp'), may hold values from 0 to 7, as said below
- trainer_qkv: float32 [2304, 3, 2048], P(('tensor', 'dp')), may hold values from -1 to 1
- trainer_out: float32 [2048, 2304], P(('tensor', 'dp')), may hold values from -0.125 to 0.125
- trainer_gate: float32 [2304, 5760], P('tensor'), may hold values from -0.125 to 0.125
- trainer_up: float32 [2304, 5760], P('tensor'), may hold values from -0.125 to 0.125
- trainer_down: float32 [2304, 5760], P('tensor'), may hold values from -0.078125 to 0.078125
- attn_gain: float32 [2304], replicated, may hold values from 0.25 to 1.75
- moe_gain: float32 [2304], replicated, may hold values from 0.25 to 1.75
- router: bfloat16 [2304, 8], replicated, may hold values from -0.125 to 0.125
Outputs:
- server_qkv: bfloat16 [2304, 3, 2048], P(None, None, 'tensor')
- server_out: bfloat16 [2048, 2304], P('tensor')
- server_gate: bfloat16 [2304, 5760], P(None, 'tensor')
- server_up: bfloat16 [2304, 5760], P(None, 'tensor')
- server_down: bfloat16 [2304, 5760], P(None, 'tensor')
- hidden_out: bfloat16 [4, 1024, 2304], P('dp', 'tensor')
- kv_cache: bfloat16 [4, 2, 1024, 2048], P('dp', None, None, 'tensor')
Inputs may be any that keep to these rules, and one draw needn't show every extreme that they name: `routes`: each row names two different experts; expert 0 is named by at most 512 rows of each prompt and by exactly 512 rows of some prompt.
All inputs are finite; a program needn't handle non-finite values. No bound on the sum of `prompt_len` on one device may be relied on, other than what follows from the above.
Results may differ from a plain program's by a relative error of at most 0.011.
The roundings to bfloat16 on the way count: a program that leaves them out, or rounds other values in their place, can miss the bound.
Values may be sent and summed in bfloat16 or wider, within the bound.
No kernel may reach another device: no remote copies, remote signals or barrier semaphores. Data moves between devices by JAX's collectives and lax.ppermute only.
A program may use at most 256 MiB of HBM per device.

v0:
```python
import jax
import jax.numpy as jnp
from jax import lax
from jax.sharding import PartitionSpec as P

HEAD_DIM = 64


def rms_scale(values, gain_row):
    mean_sq = jnp.mean(values * values, axis=-1, keepdims=True)
    return values * lax.rsqrt(mean_sq + 1e-05) * gain_row


def rotate(head_block, positions):
    half_dim = head_block.shape[-1] // 2
    inv_freq = jnp.power(
        10000.0, jnp.arange(half_dim, dtype=jnp.float32) * (-2.0 / head_block.shape[-1])
    )
    angles = positions.astype(jnp.float32)[:, None] * inv_freq[None, :]
    cosine = jnp.cos(angles)[:, None, :]
    sine_part = jnp.sin(angles)[:, None, :]
    first_half = head_block[..., :half_dim]
    second_half = head_block[..., half_dim:]
    return jnp.concatenate(
        [
            first_half * cosine - second_half * sine_part,
            second_half * cosine + first_half * sine_part,
        ],
        axis=-1,
    )


def attend_block(query_blk, key_blk, value_blk, row_start):
    scores = jnp.einsum(
        "qhd,khd->hqk", query_blk, key_blk, preferred_element_type=jnp.float32
    ) * query_blk.shape[-1] ** (-0.5)
    row_ids = row_start + jnp.arange(query_blk.shape[0], dtype=jnp.int32)
    col_ids = jnp.arange(key_blk.shape[0], dtype=jnp.int32)
    scores = jnp.where(row_ids[None, :, None] >= col_ids[None, None, :], scores, -1e30)
    row_max = jnp.max(scores, axis=-1, keepdims=True)
    exp_scores = jnp.exp(scores - row_max)
    attn_probs = (exp_scores / jnp.sum(exp_scores, axis=-1, keepdims=True)).astype(jnp.bfloat16)
    return jnp.einsum(
        "hqk,khd->qhd", attn_probs, value_blk, preferred_element_type=jnp.float32
    ).astype(jnp.bfloat16)


def shards(
    hidden_in,
    prompt_len,
    start_pos,
    routes,
    trainer_qkv,
    trainer_out,
    trainer_gate,
    trainer_up,
    trainer_down,
    attn_gain,
    moe_gain,
    router,
):
    tensor_size = lax.axis_size("tensor")
    replica_count = lax.axis_size("dp")
    expert_mats = (
        lax.all_to_all(
            trainer_gate.astype(jnp.bfloat16), "tensor", split_axis=1, concat_axis=0, tiled=True
        ),
        lax.all_to_all(
            trainer_up.astype(jnp.bfloat16), "tensor", split_axis=1, concat_axis=0, tiled=True
        ),
        lax.all_to_all(
            trainer_down.astype(jnp.bfloat16), "tensor", split_axis=1, concat_axis=0, tiled=True
        ),
    )
    server_gate, server_up, server_down = expert_mats
    qkv_cast = trainer_qkv.astype(jnp.bfloat16)
    out_cast = trainer_out.astype(jnp.bfloat16)
    column_part = lax.all_to_all(qkv_cast, "tensor", split_axis=2, concat_axis=0, tiled=True)
    stacked, server_out = (
        lax.all_gather(column_part, "dp", axis=0, tiled=True),
        lax.all_gather(out_cast, "dp", axis=0, tiled=True),
    )
    block_rows = stacked.shape[0] // (replica_count * tensor_size)
    server_qkv = (
        stacked.reshape(replica_count, tensor_size, block_rows, 3, stacked.shape[2])
        .transpose(1, 0, 2, 3, 4)
        .reshape(stacked.shape)
    )
    rows_dev = hidden_in.shape[1]
    seq_len = rows_dev * tensor_size
    length = prompt_len[0]
    offset = start_pos[0]
    my_first = lax.axis_index("tensor") * rows_dev
    tokens = hidden_in[0].astype(jnp.float32)
    normed = rms_scale(tokens, attn_gain).astype(jnp.bfloat16)
    local_width = server_qkv.shape[2]
    heads_here = local_width // HEAD_DIM
    piece = lax.all_gather(normed, "tensor", axis=0, tiled=True)
    mixed = jnp.einsum("sd,dtc->stc", piece, server_qkv, preferred_element_type=jnp.float32)
    places = offset + jnp.arange(piece.shape[0], dtype=jnp.int32)
    query_rot = rotate(mixed[:, 0].reshape(-1, heads_here, HEAD_DIM), places).reshape(
        -1, local_width
    )
    key_rot = rotate(mixed[:, 1].reshape(-1, heads_here, HEAD_DIM), places).reshape(-1, local_width)
    qkv_rows = jnp.stack([query_rot, key_rot, mixed[:, 2]], axis=1).astype(jnp.bfloat16)
    query_all = qkv_rows[:, 0].reshape(seq_len, heads_here, HEAD_DIM)
    keys_all = qkv_rows[:, 1].reshape(seq_len, heads_here, HEAD_DIM)
    values_all = qkv_rows[:, 2].reshape(seq_len, heads_here, HEAD_DIM)
    block_len = min(512, seq_len)
    block_outs = []
    for block_id in range(seq_len // block_len):
        row_lo = block_id * block_len
        row_hi = row_lo + block_len
        query_blk = query_all[row_lo:row_hi]
        key_blk = keys_all[:row_hi]
        value_blk = values_all[:row_hi]
        block_result = attend_block(query_blk, key_blk, value_blk, row_lo)
        block_outs.append(block_result)
    attended = jnp.concatenate(block_outs, axis=0).reshape(seq_len, local_width)
    attn_sum = lax.psum_scatter(
        jnp.dot(attended, server_out, preferred_element_type=jnp.float32).astype(jnp.bfloat16),
        "tensor",
        scatter_dimension=0,
        tiled=True,
    ).astype(jnp.float32)
    middle = (tokens + attn_sum).astype(jnp.bfloat16)
    normed_moe = rms_scale(middle.astype(jnp.float32), moe_gain).astype(jnp.bfloat16)
    local_routes = lax.dynamic_slice_in_dim(routes[0], my_first, rows_dev, 0)
    local_valid = my_first + jnp.arange(rows_dev, dtype=jnp.int32) < length
    logits = jnp.dot(normed_moe, router, preferred_element_type=jnp.float32)
    expert_ids = jnp.arange(router.shape[1], dtype=jnp.int32)
    logit_first = jnp.sum(
        jnp.where(local_routes[:, 0:1] == expert_ids[None, :], logits, 0.0), axis=1
    )
    logit_second = jnp.sum(
        jnp.where(local_routes[:, 1:2] == expert_ids[None, :], logits, 0.0), axis=1
    )
    other_logit = jnp.where(local_routes[:, 0] == 0, logit_second, logit_first)
    local_routed = jnp.any(local_routes == 0, axis=1)
    route_w = jnp.where(local_routed, jax.nn.sigmoid(logits[:, 0] - other_logit), 0.0)
    gathered = lax.all_gather(normed_moe, "tensor", axis=0, tiled=True)
    seq_ids = jnp.arange(seq_len, dtype=jnp.int32)
    all_routed = jnp.any(routes[0] == 0, axis=1)
    capacity = seq_len // 2
    slot = jnp.cumsum(all_routed.astype(jnp.int32)) - 1
    slot_rows = (
        jnp.full((capacity,), seq_len, jnp.int32)
        .at[jnp.where(all_routed, slot, capacity)]
        .set(seq_ids, mode="drop")
    )
    picked = gathered[jnp.minimum(slot_rows, seq_len - 1)]
    gate_val = jnp.dot(picked, server_gate, preferred_element_type=jnp.float32)
    up_val = jnp.dot(picked, server_up, preferred_element_type=jnp.float32)
    act = (jax.nn.silu(gate_val) * up_val).astype(jnp.bfloat16)
    slot_sums = lax.dot_general(
        act, server_down, (((1,), (1,)), ((), ())), preferred_element_type=jnp.float32
    )
    terms = (
        jnp.zeros((seq_len, normed_moe.shape[1]), jnp.float32)
        .at[slot_rows]
        .add(slot_sums, mode="drop")
    )
    expert_sum = lax.psum_scatter(
        terms.astype(jnp.bfloat16), "tensor", scatter_dimension=0, tiled=True
    ).astype(jnp.float32)
    result = middle.astype(jnp.float32) + route_w[:, None] * expert_sum
    hidden_out = jnp.where(local_valid[:, None], result, 0.0).astype(jnp.bfloat16)[None]
    seq_valid = jnp.arange(seq_len, dtype=jnp.int32) < length
    cache_pair = jnp.where(
        seq_valid[None, :, None], qkv_rows[:, 1:3].transpose(1, 0, 2), jnp.zeros((), jnp.bfloat16)
    )
    return (
        server_qkv,
        server_out,
        server_gate,
        server_up,
        server_down,
        hidden_out,
        cache_pair[None],
    )


def solution(mesh):
    placed = (
        P("dp", "tensor", None),
        P("dp"),
        P("dp"),
        P("dp", None, None),
        P(("tensor", "dp"), None, None),
        P(("tensor", "dp"), None),
        P("tensor", None),
        P("tensor", None),
        P("tensor", None),
        P(),
        P(),
        P(),
    )
    return jax.shard_map(
        shards,
        mesh=mesh,
        in_specs=placed,
        out_specs=(
            P(None, None, "tensor"),
            P("tensor", None),
            P(None, "tensor"),
            P(None, "tensor"),
            P(None, "tensor"),
            P("dp", "tensor", None),
            P("dp", None, None, "tensor"),
        ),
        check_vma=False,
    )
```

profile of v0, /device:TPU:0, one launch (start us, length us, event | category | flops | bytes accessed | tf_op | source)
XLA Modules:
  0.0 508.5 jit_solution(11771919291552511364)
XLA Ops:
  16.3 18.9 %all_to_all.75 = bf16[8,2,27648]{2,1,0:T(2,128)(2,1)} all-to-all(bf16[8,2,27648]{2,1,0:T(2,128)(2,1)} %reshape.272), channel_id=1, replica_groups=mesh['dp'=4,'tensor'=8] {'tensor'}, dimensions={0} | all-to-all | bytes 1769472 | tf_op jit(solution)/shard_map/all_to_all | solution.py:78
  46.1 65.7 %all-gather.5.cloned.1.call-done = bf16[2304,3,256]{2,0,1:T(8,128)(2,1)} async-done(((bf16[576,3,256]{2,0,1:T(8,128)(2,1)}), bf16[2304,3,256]{2,0,1:T(8,128)(2,1)}) %all-gather.5.cloned.1.call-update) | async-done | bytes 3538960 | tf_op jit(solution)/shard_map/all_gather | solution.py:80
  115.9 35.8 %all-gather.9.cloned.1.call-done = bf16[1024,2304]{1,0:T(8,128)(2,1)} async-done(((bf16[128,2304]{1,0:T(8,128)(2,1)}), bf16[1024,2304]{1,0:T(8,128)(2,1)}) %all-gather.9.cloned.1.call-update) | async-done | bytes 4718608 | tf_op jit(solution)/shard_map/all_gather | solution.py:98
  151.8 6.8 %fusion.61 = (bf16[1024,3,256]{0,2,1:T(8,128)(2,1)S(1)}, f32[1024,3,256]{0,2,1:T(8,128)S(1)}) fusion(bf16[2304,3,256]{2,0,1:T(8,128)(2,1)} %bitcast.102, bf16[1024,2304]{1,0:T(8,128)(2,1)} %all-gather.9.cloned.1.call-done), kind=kOutput, calls=%fused_computation.108 | convolution fusion | flops 3624665088 | bytes 12976128 | tf_op jit(solution)/shard_map/sd,dtc->stc/dot_general | solution.py:99
  159.2 5.4 %fusion.62 = (f32[4,512]{1,0:T(4,128)S(1)}, f32[4,512,1024]{2,1,0:T(8,128)}) fusion(pred[512,1024]{1,0:T(8,128)(4,1)S(1)} %iota_compare_fusion, bf16[1024,4,32]{0,2,1:T(8,128)(2,1)S(1)} %get-tuple-element.52, bf16[1024,4,32]{0,2,1:T(8,128)(2,1)S(1)} %get-tuple-element.53, bf16[1024,4,32]{0,2,1:T(8,128)(2,1)S(1)} %get-tuple-element.49, ...), kind=kOutput, calls=%fused_computation.109 | convolution fusion | flops 278397952 | bytes 9969664 | tf_op jit(solution)/shard_map/sub | solution.py:41
  174.5 10.0 %all-gather.7.cloned.1.call-done = bf16[256,2304]{1,0:T(8,128)(2,1)} async-done(((bf16[64,2304]{1,0:T(8,128)(2,1)}), bf16[256,2304]{1,0:T(8,128)(2,1)}) %all-gather.7.cloned.1.call-update) | async-done | bytes 1179664 | tf_op jit(solution)/shard_map/all_gather | solution.py:81
  184.4 4.8 convolution_convert_fusion
  189.9 52.6 %reduce-scatter.3.cloned.1.call-done = bf16[128,2304]{1,0:T(8,128)(2,1)} async-done(((bf16[1024,2304]{1,0:T(8,128)(2,1)}), bf16[128,2304]{1,0:T(8,128)(2,1)}) %reduce-scatter.3.cloned.1.call-update) | async-done | bytes 589840 | tf_op jit(solution)/shard_map/reduce_scatter | solution.py:120
  246.0 4.9 convert_element_type.88
  250.9 8.5 %all_to_all.59 = bf16[288,8,720]{2,1,0:T(8,128)(2,1)} reshape(bf16[288,5760]{1,0:T(8,128)(2,1)} %convert_element_type.88) | data formatting | bytes 6635520 | tf_op jit(solution)/shard_map/all_to_all | solution.py:65
  259.4 4.6 copy.63
  264.0 4.5 all-to-all-start.1
  268.4 5.0 convert_element_type.89
  273.4 8.5 %all_to_all.63 = bf16[288,8,720]{2,1,0:T(8,128)(2,1)} reshape(bf16[288,5760]{1,0:T(8,128)(2,1)} %convert_element_type.89) | data formatting | bytes 6635520 | tf_op jit(solution)/shard_map/all_to_all | solution.py:68
  286.4 35.8 %all-to-all-done.1 = bf16[288,8,720]{2,0,1:T(8,128)(2,1)} async-done(((bf16[288,8,720]{2,0,1:T(8,128)(2,1)}), bf16[288,8,720]{2,0,1:T(8,128)(2,1)}, u32[]{:S(2)}, u32[]{:S(2)}) %all-to-all-start.1) | async-done | bytes 3317792 | tf_op jit(solution)/shard_map/all_to_all | solution.py:65
  322.2 4.5 all-to-all-start.2
  326.7 4.9 convert_element_type.90
  331.6 8.4 %all_to_all.67 = bf16[288,8,720]{2,1,0:T(8,128)(2,1)} reshape(bf16[288,5760]{1,0:T(8,128)(2,1)} %convert_element_type.90) | data formatting | bytes 6635520 | tf_op jit(solution)/shard_map/all_to_all | solution.py:71
  340.1 4.6 copy.65
  344.6 24.2 %all-to-all-done.2 = bf16[288,8,720]{2,0,1:T(8,128)(2,1)} async-done(((bf16[288,8,720]{2,0,1:T(8,128)(2,1)}), bf16[288,8,720]{2,0,1:T(8,128)(2,1)}, u32[]{:S(2)}, u32[]{:S(2)}) %all-to-all-start.2) | async-done | bytes 3317792 | tf_op jit(solution)/shard_map/all_to_all | solution.py:68
  368.8 4.5 all-to-all-start.3
  374.0 4.5 scatter_custom_fusion
  378.5 7.8 %gather_fusion = bf16[512,2304]{1,0:T(8,128)(2,1)S(1)} fusion(bf16[1024,2304]{1,0:T(8,128)(2,1)} %all-gather.11.cloned.1.call-done, s32[1024]{0:T(1024)S(1)} %pad_clamp_fusion), kind=kCustom, calls=%fused_computation | custom fusion | bytes 4720640 | tf_op jit(solution)/shard_map/gather | solution.py:151
  386.4 5.0 fusion.72
  391.4 24.0 %all-to-all-done.3 = bf16[288,8,720]{2,0,1:T(8,128)(2,1)} async-done(((bf16[288,8,720]{2,0,1:T(8,128)(2,1)}), bf16[288,8,720]{2,0,1:T(8,128)(2,1)}, u32[]{:S(2)}, u32[]{:S(2)}) %all-to-all-start.3) | async-done | bytes 3317792 | tf_op jit(solution)/shard_map/all_to_all | solution.py:71
  415.4 9.9 %fusion.32 = f32[512,2304]{1,0:T(8,128)} fusion(bf16[2304,720]{1,0:T(8,128)(2,1)} %bitcast.12, f32[512,720]{0,1:T(8,128)} %fusion.72, bf16[512,2304]{1,0:T(8,128)(2,1)S(1)} %gather_fusion, bf16[2304,720]{1,0:T(8,128)(2,1)} %bitcast.10), kind=kOutput, calls=%fused_computation.51 | convolution fusion | flops 3399598080 | bytes 15187968 | tf_op jit(solution)/shard_map/dot_general | solution.py:155
  425.3 13.3 %scatter_custom_fusion.1 = f32[1024,2304]{1,0:T(8,128)} fusion(s32[512]{0:T(512)S(1)} %get-tuple-element.57, f32[512,2304]{1,0:T(8,128)} %fusion.32, f32[]{:T(128)} %constant.20.clone.1), kind=kCustom, calls=%fused_computation.12 | custom fusion | flops 1179648 | bytes 9437696 | tf_op jit(solution)/shard_map/scatter-add | solution.py:161
  438.6 6.4 %convert_element_type.109 = bf16[1024,2304]{1,0:T(8,128)(2,1)} convert(f32[1024,2304]{1,0:T(8,128)} %scatter_custom_fusion.1) | non-fusion elementwise | flops 2359296 | bytes 14155776 | tf_op jit(solution)/shard_map/convert_element_type | solution.py:164
  445.7 5.7 %copy.68 = bf16[2304,720]{0,1:T(8,128)(2,1)} copy(bf16[2304,720]{1,0:T(8,128)(2,1)} %bitcast.8) | data formatting | bytes 6635520
  451.4 5.9 %copy.69 = bf16[2304,720]{0,1:T(8,128)(2,1)} copy(bf16[2304,720]{1,0:T(8,128)(2,1)} %bitcast.10) | data formatting | bytes 6635520
  457.3 5.7 %copy.70 = bf16[2304,720]{0,1:T(8,128)(2,1)} copy(bf16[2304,720]{1,0:T(8,128)(2,1)} %bitcast.12) | data formatting | bytes 6635520
  466.8 31.4 %reduce-scatter.5.cloned.1.call-done = bf16[128,2304]{1,0:T(8,128)(2,1)} async-done(((bf16[1024,2304]{1,0:T(8,128)(2,1)}), bf16[128,2304]{1,0:T(8,128)(2,1)}) %reduce-scatter.5.cloned.1.call-update) | async-done | bytes 589840 | tf_op jit(solution)/shard_map/reduce_scatter | solution.py:163
  (91 shorter events, 50.1 us)
Async XLA Ops:
  7.2 459.3 %copy-start = (bf16[2304,8]{0,1:T(8,128)(2,1)S(1)}, bf16[2304,8]{0,1:T(8,128)(2,1)}, u32[]{:S(2)}) copy-start(bf16[2304,8]{0,1:T(8,128)(2,1)} %param.23) | copy-start | bytes 110596
  7.2 104.6 %all-gather.5.cloned.1.call-start = ((), (), s32[]{:S(2)}) async-start(), calls=%async_computation.6 | async-start | bytes 4423680 | tf_op jit(solution)/shard_map/all_gather | solution.py:80
  35.2 6.8 %copy-start.1 = (bf16[1,128,2304]{2,1,0:T(8,128)(2,1)S(1)}, bf16[1,128,2304]{2,1,0:T(8,128)(2,1)}, u32[]{:S(2)}) copy-start(bf16[1,128,2304]{2,1,0:T(8,128)(2,1)} %param.12) | copy-start | bytes 1769476
  35.2 7.0 %copy-start.10 = (f32[2304]{0:T(1024)S(1)}, f32[2304]{0:T(1024)}, u32[]{:S(2)}) copy-start(f32[2304]{0:T(1024)} %param.21) | copy-start | bytes 27652
  39.7 3.6 copy-start.9
  41.9 109.9 %all-gather.9.cloned.1.call-start = ((), (), s32[]{:S(2)}) async-start(), calls=%async_computation.8 | async-start | bytes 5308416 | tf_op jit(solution)/shard_map/all_gather | solution.py:98
  43.2 141.2 %all-gather.7.cloned.1.call-start = ((), (), s32[]{:S(2)}) async-start(), calls=%async_computation.7 | async-start | bytes 1474560 | tf_op jit(solution)/shard_map/all_gather | solution.py:81
  44.1 198.4 %reduce-scatter.3.cloned.1.call-start = ((), (), s32[]{:S(2)}) async-start(), calls=%async_computation.9 | async-start | bytes 5308416 | tf_op jit(solution)/shard_map/reduce_scatter | solution.py:120
  159.2 5.4 %copy-start.5 = (bf16[1024,4,32]{0,2,1:T(8,128)(2,1)}, bf16[1024,4,32]{0,2,1:T(8,128)(2,1)S(1)}, u32[]{:S(2)}) copy-start(bf16[1024,4,32]{0,2,1:T(8,128)(2,1)S(1)} %get-tuple-element.48) | copy-start | bytes 786436
  159.2 5.4 %copy-start.7 = (bf16[1024,4,32]{0,2,1:T(8,128)(2,1)}, bf16[1024,4,32]{0,2,1:T(8,128)(2,1)S(1)}, u32[]{:S(2)}) copy-start(bf16[1024,4,32]{0,2,1:T(8,128)(2,1)S(1)} %get-tuple-element.49) | copy-start | bytes 786436
  168.2 4.7 copy-start.13
  189.3 54.5 %copy-start.11 = (f32[2304]{0:T(1024)S(1)}, f32[2304]{0:T(1024)}, u32[]{:S(2)}) copy-start(f32[2304]{0:T(1024)} %param.22) | copy-start | bytes 27652
  189.3 189.2 %all-gather.11.cloned.1.call-start = ((), (), s32[]{:S(2)}) async-start(), calls=%async_computation.10 | async-start | bytes 5308416 | tf_op jit(solution)/shard_map/all_gather | solution.py:141
  264.0 58.2 %all-to-all-start.1 = ((bf16[288,8,720]{2,0,1:T(8,128)(2,1)}), bf16[288,8,720]{2,0,1:T(8,128)(2,1)}, u32[]{:S(2)}, u32[]{:S(2)}) async-start(bf16[288,8,720]{2,0,1:T(8,128)(2,1)} %copy.63), calls=%async_computation.1 | async-start | bytes 7077888 | tf_op jit(solution)/shard_map/all_to_all | solution.py:65
  322.2 46.6 %all-to-all-start.2 = ((bf16[288,8,720]{2,0,1:T(8,128)(2,1)}), bf16[288,8,720]{2,0,1:T(8,128)(2,1)}, u32[]{:S(2)}, u32[]{:S(2)}) async-start(bf16[288,8,720]{2,0,1:T(8,128)(2,1)} %copy.64), calls=%async_computation.2 | async-start | bytes 7077888 | tf_op jit(solution)/shard_map/all_to_all | solution.py:68
  344.6 28.7 %copy-start.12 = (s32[1,1024,2]{1,2,0:T(2,128)S(1)}, s32[1,1024,2]{1,2,0:T(2,128)}, u32[]{:S(2)}) copy-start(s32[1,1024,2]{1,2,0:T(2,128)} %param.15) | copy-start | bytes 24580
  368.8 46.6 %all-to-all-start.3 = ((bf16[288,8,720]{2,0,1:T(8,128)(2,1)}), bf16[288,8,720]{2,0,1:T(8,128)(2,1)}, u32[]{:S(2)}, u32[]{:S(2)}) async-start(bf16[288,8,720]{2,0,1:T(8,128)(2,1)} %copy.65), calls=%async_computation.3 | async-start | bytes 7077888 | tf_op jit(solution)/shard_map/all_to_all | solution.py:71
  373.3 124.9 %reduce-scatter.5.cloned.1.call-start = ((), (), s32[]{:S(2)}) async-start(), calls=%async_computation.11 | async-start | bytes 5308416 | tf_op jit(solution)/shard_map/reduce_scatter | solution.py:163
  457.3 5.7 %copy-start.6 = (bf16[1024,4,32]{0,2,1:T(8,128)(2,1)S(1)}, bf16[1024,4,32]{0,2,1:T(8,128)(2,1)}, u32[]{:S(2)}) copy-start(bf16[1024,4,32]{0,2,1:T(8,128)(2,1)} %copy-done.5) | copy-start | bytes 786436
  457.3 5.7 %copy-start.8 = (bf16[1024,4,32]{0,2,1:T(8,128)(2,1)S(1)}, bf16[1024,4,32]{0,2,1:T(8,128)(2,1)}, u32[]{:S(2)}) copy-start(bf16[1024,4,32]{0,2,1:T(8,128)(2,1)} %copy-done.7) | copy-start | bytes 786436
  463.1 3.4 copy-start.2
  463.1 35.1 %copy-start.3 = (bf16[128,2304]{1,0:T(8,128)(2,1)S(1)}, bf16[128,2304]{1,0:T(8,128)(2,1)}, u32[]{:S(2)}) copy-start(bf16[128,2304]{1,0:T(8,128)(2,1)} %reduce-scatter.3.cloned.1.call-done) | copy-start | bytes 1769476
  463.1 37.3 %copy-start.4 = (bf16[256,2304]{1,0:T(8,128)(2,1)S(1)}, bf16[256,2304]{1,0:T(8,128)(2,1)}, u32[]{:S(2)}) copy-start(bf16[256,2304]{1,0:T(8,128)(2,1)} %all-gather.7.cloned.1.call-done) | copy-start | bytes 3538948
Sparse Core Ops, SparseCore 0:
  42.0 69.6 all-gather.4
  114.2 37.5 all-gather.8
  153.9 30.4 all-gather.6
  189.4 52.9 reduce-scatter.2
  246.1 60.3 all-gather.10
  445.1 53.0 reduce-scatter.4
where the time goes:
time: 513 us; the launch traced here: 509 us
  waiting for transfers between devices  279 us (54%)
  local copies, waits for them, and re-layouts  91.6 us (18%)
  other arithmetic  47.8 us (9%)
  matrix products  40.3 us (8%)
  blocking collectives  18.9 us (4%)
  between operations  16 us (3%)
  starting transfers between devices  14.5 us (3%)
    all_gather x1, waiting for transfers between devices, shards(): lax.all_gather(column_part, 'dp', axis=0, tiled=True)  65.7 us
    reduce_scatter x1, waiting for transfers between devices, shards(): lax.psum_scatter(jnp.dot(attended, server_out, preferred_element_type=jnp...  52.6 us
    all_gather x1, waiting for transfers between devices, shards(): piece = lax.all_gather(normed, 'tensor', axis=0, tiled=True)  35.8 us
    all_to_all x1, waiting for transfers between devices, shards(): lax.all_to_all(trainer_gate.astype(jnp.bfloat16), 'tensor', split_axis=1,...  35.8 us
    reduce_scatter x1, waiting for transfers between devices, shards(): lax.psum_scatter(terms.astype(jnp.bfloat16), 'tensor', scatter_dimension=...  31.4 us
    unnamed x35, local copies, waits for them, and re-layouts  30.7 us
    all_to_all x1, waiting for transfers between devices, shards(): lax.all_to_all(trainer_up.astype(jnp.bfloat16), 'tensor', split_axis=1, c...  24.2 us
    all_to_all x1, waiting for transfers between devices, shards(): lax.all_to_all(trainer_down.astype(jnp.bfloat16), 'tensor', split_axis=1,...  24 us
  transfers between devices with their start and end apart: 9, of which 8 were waited for; matrix products, arithmetic and copies ran while one was open for 19% of the time, Pallas kernels for 0%

commit v1 on v0

--- a/solution.py
+++ b/solution.py
@@ -77,7 +77,9 @@
     out_cast = trainer_out.astype(jnp.bfloat16)
     column_part = lax.all_to_all(qkv_cast, "tensor", split_axis=2, concat_axis=0, tiled=True)
     stacked, server_out = (
-        lax.all_gather(column_part, "dp", axis=0, tiled=True),
+        jnp.concatenate(
+            lax.all_to_all(jnp.stack([column_part] * lax.axis_size("dp")), "dp", 0, 0), axis=0
+        ),
         lax.all_gather(out_cast, "dp", axis=0, tiled=True),
     )
     block_rows = stacked.shape[0] // (replica_count * tensor_size)

time: 513 us -> 509 us (level)
  waiting for transfers between devices: 279 us -> 261 us
    all_to_all x0 -> x1, waiting for transfers between devices: none -> 94.8 us  [shards(): lax.all_to_all(jnp.stack([column_part] * lax.axis_size('dp')), 'dp', 0, 0)]
    all_gather x1 -> x0, waiting for transfers between devices: 65.7 us -> none  [shards(): lax.all_gather(column_part, 'dp', axis=0, tiled=True)]
    all_gather x1, waiting for transfers between devices: 35.8 us -> 0.01 us  [shards(): piece = lax.all_gather(normed, 'tensor', axis=0, tiled=True)]
    all_gather x1, waiting for transfers between devices: 9.96 us -> 0.02 us  [shards(): lax.all_gather(out_cast, 'dp', axis=0, tiled=True)]
    unnamed x35 -> x39, local copies, waits for them, and re-layouts: 30.7 us -> 30.7 us
  transfers between devices with their start and end apart: 9 -> 9, of which waited for: 8 -> 6; matrix products, arithmetic and copies ran while one was open for 19% -> 22% of each run, Pallas kernels for 0% -> 0%
where the time goes in v1:
time: 509 us; the launch traced here: 504 us
  waiting for transfers between devices  261 us (51%)
  local copies, waits for them, and re-layouts  95.6 us (19%)
  other arithmetic  49.2 us (10%)
  matrix products  40.2 us (8%)
  blocking collectives  22.3 us (4%)
  starting transfers between devices  19.3 us (4%)
  between operations  15.7 us (3%)
    all_to_all x1, waiting for transfers between devices, shards(): lax.all_to_all(jnp.stack([column_part] * lax.axis_size('dp')), 'dp', 0, 0)  94.8 us
    reduce_scatter x1, waiting for transfers between devices, shards(): lax.psum_scatter(jnp.dot(attended, server_out, preferred_element_type=jnp...  51.3 us
    all_to_all x1, waiting for transfers between devices, shards(): lax.all_to_all(trainer_gate.astype(jnp.bfloat16), 'tensor', split_axis=1,...  35.8 us
    reduce_scatter x1, waiting for transfers between devices, shards(): lax.psum_scatter(terms.astype(jnp.bfloat16), 'tensor', scatter_dimension=...  31.4 us
    unnamed x39, local copies, waits for them, and re-layouts  30.7 us
    all_to_all x1, waiting for transfers between devices, shards(): lax.all_to_all(trainer_up.astype(jnp.bfloat16), 'tensor', split_axis=1, c...  24.2 us
    all_to_all x1, waiting for transfers between devices, shards(): lax.all_to_all(trainer_down.astype(jnp.bfloat16), 'tensor', split_axis=1,...  24 us
    all_to_all x1, blocking collectives, shards(): lax.all_to_all(qkv_cast, 'tensor', split_axis=2, concat_axis=0, tiled=True)  22.3 us
  transfers between devices with their start and end apart: 9, of which 6 were waited for; matrix products, arithmetic and copies ran while one was open for 22% of the time, Pallas kernels for 0%

profile of v1, /device:TPU:0, one launch (start us, length us, event | category | flops | bytes accessed | tf_op | source)
XLA Modules:
  0.0 503.8 jit_solution(7496581908609579405)
XLA Ops:
  18.4 22.3 %all_to_all.77 = bf16[8,2,27648]{2,1,0:T(2,128)(2,1)} all-to-all(bf16[8,2,27648]{2,1,0:T(2,128)(2,1)} %reshape.271), channel_id=1, replica_groups=mesh['dp'=4,'tensor'=8] {'tensor'}, dimensions={0} | all-to-all | bytes 1769472 | tf_op jit(solution)/shard_map/all_to_all | solution.py:78
  40.6 4.5 reshape.272
  50.6 4.9 all-to-all-start.1
  59.0 94.8 %all-to-all-done.1 = bf16[4,576,3,256]{3,1,2,0:T(8,128)(2,1)} async-done(((bf16[4,576,3,256]{3,1,2,0:T(8,128)(2,1)}), bf16[4,576,3,256]{3,1,2,0:T(8,128)(2,1)}, u32[]{:S(2)}, u32[]{:S(2)}) %all-to-all-start.1) | async-done | bytes 3538976 | tf_op jit(solution)/shard_map/all_to_all | solution.py:81
  158.0 6.8 %fusion.61 = (bf16[1024,3,256]{0,2,1:T(8,128)(2,1)S(1)}, f32[1024,3,256]{0,2,1:T(8,128)S(1)}) fusion(bf16[2304,3,256]{2,0,1:T(8,128)(2,1)} %bitcast.102, bf16[1024,2304]{1,0:T(8,128)(2,1)} %all-gather.6.cloned.1.call-done), kind=kOutput, calls=%fused_computation.108 | convolution fusion | flops 3624665088 | bytes 12976128 | tf_op jit(solution)/shard_map/sd,dtc->stc/dot_general | solution.py:101
  166.1 5.4 %fusion.62 = (f32[4,512]{1,0:T(4,128)S(1)}, f32[4,512,1024]{2,1,0:T(8,128)}) fusion(pred[512,1024]{1,0:T(8,128)(4,1)S(1)} %iota_compare_fusion, bf16[1024,4,32]{0,2,1:T(8,128)(2,1)S(1)} %get-tuple-element.52, bf16[1024,4,32]{0,2,1:T(8,128)(2,1)S(1)} %get-tuple-element.53, bf16[1024,4,32]{0,2,1:T(8,128)(2,1)S(1)} %get-tuple-element.49, ...), kind=kOutput, calls=%fused_computation.109 | convolution fusion | flops 278397952 | bytes 9969664 | tf_op jit(solution)/shard_map/sub | solution.py:41
  181.4 4.8 convolution_convert_fusion
  186.8 51.3 %reduce-scatter.3.cloned.1.call-done = bf16[128,2304]{1,0:T(8,128)(2,1)} async-done(((bf16[1024,2304]{1,0:T(8,128)(2,1)}), bf16[128,2304]{1,0:T(8,128)(2,1)}) %reduce-scatter.3.cloned.1.call-update) | async-done | bytes 589840 | tf_op jit(solution)/shard_map/reduce_scatter | solution.py:122
  241.6 4.9 convert_element_type.88
  246.6 8.5 %all_to_all.60 = bf16[288,8,720]{2,1,0:T(8,128)(2,1)} reshape(bf16[288,5760]{1,0:T(8,128)(2,1)} %convert_element_type.88) | data formatting | bytes 6635520 | tf_op jit(solution)/shard_map/all_to_all | solution.py:65
  255.1 4.6 copy.63
  259.6 4.5 all-to-all-start.2
  264.1 5.0 convert_element_type.89
  269.1 8.5 %all_to_all.64 = bf16[288,8,720]{2,1,0:T(8,128)(2,1)} reshape(bf16[288,5760]{1,0:T(8,128)(2,1)} %convert_element_type.89) | data formatting | bytes 6635520 | tf_op jit(solution)/shard_map/all_to_all | solution.py:68
  282.0 35.8 %all-to-all-done.2 = bf16[288,8,720]{2,0,1:T(8,128)(2,1)} async-done(((bf16[288,8,720]{2,0,1:T(8,128)(2,1)}), bf16[288,8,720]{2,0,1:T(8,128)(2,1)}, u32[]{:S(2)}, u32[]{:S(2)}) %all-to-all-start.2) | async-done | bytes 3317792 | tf_op jit(solution)/shard_map/all_to_all | solution.py:65
  317.8 4.5 all-to-all-start.3
  322.3 4.9 convert_element_type.90
  327.3 8.4 %all_to_all.68 = bf16[288,8,720]{2,1,0:T(8,128)(2,1)} reshape(bf16[288,5760]{1,0:T(8,128)(2,1)} %convert_element_type.90) | data formatting | bytes 6635520 | tf_op jit(solution)/shard_map/all_to_all | solution.py:71
  335.7 4.6 copy.65
  340.3 24.2 %all-to-all-done.3 = bf16[288,8,720]{2,0,1:T(8,128)(2,1)} async-done(((bf16[288,8,720]{2,0,1:T(8,128)(2,1)}), bf16[288,8,720]{2,0,1:T(8,128)(2,1)}, u32[]{:S(2)}, u32[]{:S(2)}) %all-to-all-start.3) | async-done | bytes 3317792 | tf_op jit(solution)/shard_map/all_to_all | solution.py:68
  364.4 4.5 all-to-all-start.4
  369.6 4.5 scatter_custom_fusion
  374.2 7.8 %gather_fusion = bf16[512,2304]{1,0:T(8,128)(2,1)S(1)} fusion(bf16[1024,2304]{1,0:T(8,128)(2,1)} %all-gather.8.cloned.1.call-done, s32[1024]{0:T(1024)S(1)} %pad_clamp_fusion), kind=kCustom, calls=%fused_computation | custom fusion | bytes 4720640 | tf_op jit(solution)/shard_map/gather | solution.py:153
  382.0 5.0 %fusion.72 = f32[512,720]{0,1:T(8,128)} fusion(bf16[512,2304]{1,0:T(8,128)(2,1)S(1)} %gather_fusion, bf16[2304,720]{1,0:T(8,128)(2,1)} %bitcast.8), kind=kOutput, calls=%fused_computation.111 | convolution fusion | flops 1698693120 | bytes 7151616 | tf_op jit(solution)/shard_map/dot_general | solution.py:154
  387.1 24.0 %all-to-all-done.4 = bf16[288,8,720]{2,0,1:T(8,128)(2,1)} async-done(((bf16[288,8,720]{2,0,1:T(8,128)(2,1)}), bf16[288,8,720]{2,0,1:T(8,128)(2,1)}, u32[]{:S(2)}, u32[]{:S(2)}) %all-to-all-start.4) | async-done | bytes 3317792 | tf_op jit(solution)/shard_map/all_to_all | solution.py:71
  411.0 9.9 %fusion.32 = f32[512,2304]{1,0:T(8,128)} fusion(bf16[2304,720]{1,0:T(8,128)(2,1)} %bitcast.12, f32[512,720]{0,1:T(8,128)} %fusion.72, bf16[512,2304]{1,0:T(8,128)(2,1)S(1)} %gather_fusion, bf16[2304,720]{1,0:T(8,128)(2,1)} %bitcast.10), kind=kOutput, calls=%fused_computation.51 | convolution fusion | flops 3399598080 | bytes 15187968 | tf_op jit(solution)/shard_map/dot_general | solution.py:157
  421.0 13.3 %scatter_custom_fusion.1 = f32[1024,2304]{1,0:T(8,128)} fusion(s32[512]{0:T(512)S(1)} %get-tuple-element.57, f32[512,2304]{1,0:T(8,128)} %fusion.32, f32[]{:T(128)} %constant.20.clone.1), kind=kCustom, calls=%fused_computation.12 | custom fusion | flops 1179648 | bytes 9437696 | tf_op jit(solution)/shard_map/scatter-add | solution.py:163
  434.2 6.4 %convert_element_type.109 = bf16[1024,2304]{1,0:T(8,128)(2,1)} convert(f32[1024,2304]{1,0:T(8,128)} %scatter_custom_fusion.1) | non-fusion elementwise | flops 2359296 | bytes 14155776 | tf_op jit(solution)/shard_map/convert_element_type | solution.py:166
  441.4 5.7 %copy.68 = bf16[2304,720]{0,1:T(8,128)(2,1)} copy(bf16[2304,720]{1,0:T(8,128)(2,1)} %bitcast.8) | data formatting | bytes 6635520
  447.1 5.9 %copy.69 = bf16[2304,720]{0,1:T(8,128)(2,1)} copy(bf16[2304,720]{1,0:T(8,128)(2,1)} %bitcast.10) | data formatting | bytes 6635520
  453.0 5.7 %copy.70 = bf16[2304,720]{0,1:T(8,128)(2,1)} copy(bf16[2304,720]{1,0:T(8,128)(2,1)} %bitcast.12) | data formatting | bytes 6635520
  462.5 31.4 %reduce-scatter.5.cloned.1.call-done = bf16[128,2304]{1,0:T(8,128)(2,1)} async-done(((bf16[1024,2304]{1,0:T(8,128)(2,1)}), bf16[128,2304]{1,0:T(8,128)(2,1)}) %reduce-scatter.5.cloned.1.call-update) | async-done | bytes 589840 | tf_op jit(solution)/shard_map/reduce_scatter | solution.py:165
  (95 shorter events, 51.0 us)
Async XLA Ops:
  7.2 455.0 %copy-start = (bf16[2304,8]{0,1:T(8,128)(2,1)S(1)}, bf16[2304,8]{0,1:T(8,128)(2,1)}, u32[]{:S(2)}) copy-start(bf16[2304,8]{0,1:T(8,128)(2,1)} %param.23) | copy-start | bytes 110596
  7.2 3.6 copy-start.5
  7.2 150.8 %all-gather.6.cloned.1.call-start = ((), (), s32[]{:S(2)}) async-start(), calls=%async_computation.8 | async-start | bytes 5308416 | tf_op jit(solution)/shard_map/all_gather | solution.py:100
  50.6 4.9 copy-start.10
  50.6 103.2 %all-to-all-start.1 = ((bf16[4,576,3,256]{3,1,2,0:T(8,128)(2,1)}), bf16[4,576,3,256]{3,1,2,0:T(8,128)(2,1)}, u32[]{:S(2)}, u32[]{:S(2)}) async-start(bf16[4,576,3,256]{3,1,2,0:T(8,128)(2,1)} %stack.14), calls=%async_computation.1 | async-start | bytes 7077888 | tf_op jit(solution)/shard_map/all_to_all | solution.py:81
  55.5 125.9 %all-gather.4.cloned.1.call-start = ((), (), s32[]{:S(2)}) async-start(), calls=%async_computation.7 | async-start | bytes 1474560 | tf_op jit(solution)/shard_map/all_gather | solution.py:83
  56.3 181.8 %reduce-scatter.3.cloned.1.call-start = ((), (), s32[]{:S(2)}) async-start(), calls=%async_computation.9 | async-start | bytes 5308416 | tf_op jit(solution)/shard_map/reduce_scatter | solution.py:122
  166.1 5.4 %copy-start.6 = (bf16[1024,4,32]{0,2,1:T(8,128)(2,1)}, bf16[1024,4,32]{0,2,1:T(8,128)(2,1)S(1)}, u32[]{:S(2)}) copy-start(bf16[1024,4,32]{0,2,1:T(8,128)(2,1)S(1)} %get-tuple-element.48) | copy-start | bytes 786436
  166.1 5.4 %copy-start.8 = (bf16[1024,4,32]{0,2,1:T(8,128)(2,1)}, bf16[1024,4,32]{0,2,1:T(8,128)(2,1)S(1)}, u32[]{:S(2)}) copy-start(bf16[1024,4,32]{0,2,1:T(8,128)(2,1)S(1)} %get-tuple-element.49) | copy-start | bytes 786436
  166.1 5.4 %copy-start.11 = (pred[512,512]{0,1:T(8,128)(4,1)S(1)}, pred[512,512]{0,1:T(8,128)(4,1)}, u32[]{:S(2)}) copy-start(pred[512,512]{0,1:T(8,128)(4,1)} %iota_compare_fusion.1) | copy-start | bytes 786436
  171.5 3.7 copy-start.12
  175.1 4.6 copy-start.15
  186.2 51.9 %copy-start.1 = (bf16[1,128,2304]{2,1,0:T(8,128)(2,1)S(1)}, bf16[1,128,2304]{2,1,0:T(8,128)(2,1)}, u32[]{:S(2)}) copy-start(bf16[1,128,2304]{2,1,0:T(8,128)(2,1)} %param.12) | copy-start | bytes 1769476
  186.2 53.2 %copy-start.13 = (f32[2304]{0:T(1024)S(1)}, f32[2304]{0:T(1024)}, u32[]{:S(2)}) copy-start(f32[2304]{0:T(1024)} %param.22) | copy-start | bytes 27652
  186.2 187.9 %all-gather.8.cloned.1.call-start = ((), (), s32[]{:S(2)}) async-start(), calls=%async_computation.10 | async-start | bytes 5308416 | tf_op jit(solution)/shard_map/all_gather | solution.py:143
  259.6 58.2 %all-to-all-start.2 = ((bf16[288,8,720]{2,0,1:T(8,128)(2,1)}), bf16[288,8,720]{2,0,1:T(8,128)(2,1)}, u32[]{:S(2)}, u32[]{:S(2)}) async-start(bf16[288,8,720]{2,0,1:T(8,128)(2,1)} %copy.63), calls=%async_computation.2 | async-start | bytes 7077888 | tf_op jit(solution)/shard_map/all_to_all | solution.py:65
  317.8 46.6 %all-to-all-start.3 = ((bf16[288,8,720]{2,0,1:T(8,128)(2,1)}), bf16[288,8,720]{2,0,1:T(8,128)(2,1)}, u32[]{:S(2)}, u32[]{:S(2)}) async-start(bf16[288,8,720]{2,0,1:T(8,128)(2,1)} %copy.64), calls=%async_computation.3 | async-start | bytes 7077888 | tf_op jit(solution)/shard_map/all_to_all | solution.py:68
  340.3 28.7 %copy-start.14 = (s32[1,1024,2]{1,2,0:T(2,128)S(1)}, s32[1,1024,2]{1,2,0:T(2,128)}, u32[]{:S(2)}) copy-start(s32[1,1024,2]{1,2,0:T(2,128)} %param.15) | copy-start | bytes 24580
  364.4 46.6 %all-to-all-start.4 = ((bf16[288,8,720]{2,0,1:T(8,128)(2,1)}), bf16[288,8,720]{2,0,1:T(8,128)(2,1)}, u32[]{:S(2)}, u32[]{:S(2)}) async-start(bf16[288,8,720]{2,0,1:T(8,128)(2,1)} %copy.65), calls=%async_computation.4 | async-start | bytes 7077888 | tf_op jit(solution)/shard_map/all_to_all | solution.py:71
  368.9 124.9 %reduce-scatter.5.cloned.1.call-start = ((), (), s32[]{:S(2)}) async-start(), calls=%async_computation.11 | async-start | bytes 5308416 | tf_op jit(solution)/shard_map/reduce_scatter | solution.py:165
  453.0 5.7 %copy-start.7 = (bf16[1024,4,32]{0,2,1:T(8,128)(2,1)S(1)}, bf16[1024,4,32]{0,2,1:T(8,128)(2,1)}, u32[]{:S(2)}) copy-start(bf16[1024,4,32]{0,2,1:T(8,128)(2,1)} %copy-done.6) | copy-start | bytes 786436
  453.0 5.7 %copy-start.9 = (bf16[1024,4,32]{0,2,1:T(8,128)(2,1)S(1)}, bf16[1024,4,32]{0,2,1:T(8,128)(2,1)}, u32[]{:S(2)}) copy-start(bf16[1024,4,32]{0,2,1:T(8,128)(2,1)} %copy-done.8) | copy-start | bytes 786436
  458.7 3.4 copy-start.2
  458.7 35.1 %copy-start.3 = (bf16[128,2304]{1,0:T(8,128)(2,1)S(1)}, bf16[128,2304]{1,0:T(8,128)(2,1)}, u32[]{:S(2)}) copy-start(bf16[128,2304]{1,0:T(8,128)(2,1)} %reduce-scatter.3.cloned.1.call-done) | copy-start | bytes 1769476
  458.8 37.3 %copy-start.4 = (bf16[256,2304]{1,0:T(8,128)(2,1)S(1)}, bf16[256,2304]{1,0:T(8,128)(2,1)}, u32[]{:S(2)}) copy-start(bf16[256,2304]{1,0:T(8,128)(2,1)} %all-gather.4.cloned.1.call-done) | copy-start | bytes 3538948
Sparse Core Ops, SparseCore 0:
  10.9 48.4 all-gather.5
  61.5 46.3 all-gather.3
  186.4 51.6 reduce-scatter.2
  241.7 60.3 all-gather.7
  440.8 53.0 reduce-scatter.4
